TPU v7x, 256 devices: a whole 4x4x8 slice. The times are simulated.
256 devices in a mesh: trav: 8 (over z), bulk: 32 (over y, x, core).
Axes of the slice: x: 4, y: 4, z: 8, core: 2. Of those that a mesh axis runs over, the one named last changes fastest.
Arguments:
- parents: bfloat16 [49152, 1024], P(('trav', 'bulk')), may hold values from -6 to 6
- act_table: bfloat16 [128, 1024], replicated, may hold values from -5 to 5
- bucket_table: bfloat16 [8192, 1024], P('bulk'), may hold values from -5 to 5
- w_first: bfloat16 [1024, 2048], P(('trav', 'bulk')), may hold values from -0.1875 to 0.1875
- b_first: float32 [2048], replicated, may hold values from -3 to 3
- w_second: bfloat16 [2048, 2048], P(('trav', 'bulk')), may hold values from -0.1875 to 0.1875
- b_second: float32 [2048], replicated, may hold values from -3 to 3
- w_head: bfloat16 [2048, 8], replicated, may hold values from -0.1875 to 0.1875
- b_head: float32 [8], replicated, may hold values from -3 to 3
- branch_counts: int32 [49152], P(('trav', 'bulk')), may hold values from 1 to 4
- sampled_actions: int32 [49152, 4], P(('trav', 'bulk')), may hold values from 0 to 127
- bucket_owner: int32 [49152, 1], P(('trav', 'bulk')), may hold values from 0 to 31; in each aligned block of 192 rows (0 to 191, 192 to 383, ...) at most 8 rows name the same one
- bucket_row: int32 [49152], P(('trav', 'bulk')), may hold values from 0 to 255
- legal_mask: int32 [49152, 32], P(('trav', 'bulk')), may hold values 0 or 1
- ancestor: int32 [49152], P(('trav', 'bulk')), may hold values from 0 to 47
Outputs:
- strategy: float32 [49152, 32], P(('trav', 'bulk'))
- ancestor_value: float32 [12288], P(('trav', 'bulk'))
Inputs may be any that keep to these rules, and one draw needn't show every extreme that they name: `bucket_owner`: in each aligned block of 192 histories (the histories of one device) no evaluator is named more than 8 times, a bound that some block reaches.
All inputs are finite; a program needn't handle non-finite values. No bound on the sum of `legal_mask` on one device may be relied on, other than what follows from the above.
Results may differ from a plain program's by a relative error of at most 0.0078.
Values may be sent and summed in bfloat16 or wider, within the bound.
A program may use at most 64 MiB of HBM per device.

v0:
```python
import jax
import jax.numpy as jnp
from jax import lax
from jax.sharding import PartitionSpec as P

tremble = 0.05


def network(inputs, w_first, b_first, w_second, b_second, w_head, b_head):
    columns = inputs
    first = jnp.dot(
        columns,
        lax.all_gather(w_first, ("trav", "bulk"), axis=0, tiled=True),
        preferred_element_type=jnp.float32,
    )
    hidden_one = jnp.maximum(first + b_first, 0.0).astype(jnp.bfloat16)
    columns = hidden_one
    second = jnp.dot(
        columns,
        lax.all_gather(w_second, ("trav", "bulk"), axis=0, tiled=True),
        preferred_element_type=jnp.float32,
    )
    hidden_two = jnp.maximum(second + b_second, 0.0).astype(jnp.bfloat16)
    return jnp.dot(hidden_two, w_head, preferred_element_type=jnp.float32) + b_head


def body(
    parents,
    act_table,
    bucket_table,
    w_first,
    b_first,
    w_second,
    b_second,
    w_head,
    b_head,
    branch_counts,
    sampled_actions,
    bucket_owner,
    bucket_row,
    legal_mask,
    ancestor,
):
    par_count = parents.shape[0]
    feature_count = parents.shape[1]
    branch_slots = sampled_actions.shape[1]
    vocab_size = act_table.shape[0]
    action_count = w_head.shape[1]
    bulk_count = lax.axis_size("bulk")
    capacity = max(2, (4 * par_count + 3 * bulk_count - 1) // (3 * bulk_count))
    slot_total = bulk_count * capacity
    action_onehot = (
        sampled_actions.reshape(-1)[:, None] == jnp.arange(vocab_size)[None, :]
    ).astype(jnp.bfloat16)
    act_rows = jnp.dot(action_onehot, act_table, preferred_element_type=jnp.float32)
    base = (jnp.repeat(parents.astype(jnp.float32), branch_slots, axis=0) + act_rows).astype(
        jnp.bfloat16
    )
    base = lax.optimization_barrier(base)
    owner_index = bucket_owner[:, 0]
    owner_hits = (owner_index[:, None] == jnp.arange(bulk_count)[None, :]).astype(jnp.int32)
    earlier = jnp.cumsum(owner_hits, axis=0) - owner_hits
    slot_index = owner_index * capacity + jnp.sum(earlier * owner_hits, axis=1)
    placement_int = (slot_index[None, :] == jnp.arange(slot_total)[:, None]).astype(jnp.int32)
    slot_bucket = jnp.sum(placement_int * bucket_row[None, :], axis=1).reshape(bulk_count, capacity)
    placement = placement_int.astype(jnp.bfloat16)
    outgoing = jnp.dot(
        placement,
        base.reshape(par_count, branch_slots * feature_count),
        preferred_element_type=jnp.float32,
    )
    outgoing = outgoing.astype(jnp.bfloat16).reshape(
        bulk_count, capacity * branch_slots, feature_count
    )
    arrived_rows = lax.all_to_all(outgoing, "bulk", split_axis=0, concat_axis=0, tiled=True)
    arrived_ids = lax.all_to_all(slot_bucket, "bulk", split_axis=0, concat_axis=0, tiled=True)
    table_rows = jnp.take(bucket_table, arrived_ids.reshape(-1), axis=0)
    inputs = (
        arrived_rows.reshape(slot_total, branch_slots, feature_count).astype(jnp.float32)
        + table_rows.astype(jnp.float32)[:, None, :]
    )
    inputs = inputs.astype(jnp.bfloat16).reshape(slot_total * branch_slots, feature_count)
    evaluated = network(inputs, w_first, b_first, w_second, b_second, w_head, b_head)
    returned = lax.all_to_all(
        evaluated.reshape(bulk_count, capacity * branch_slots * action_count).astype(jnp.bfloat16),
        "bulk",
        split_axis=0,
        concat_axis=0,
        tiled=True,
    ).astype(jnp.float32)
    advantage = jnp.take(
        returned.reshape(slot_total, branch_slots * action_count), slot_index, axis=0
    )
    advantage = advantage.reshape(par_count, branch_slots, action_count)
    first_action = (jnp.arange(action_count) == 0).astype(jnp.float32)
    allowed = jnp.maximum(
        legal_mask.reshape(par_count, branch_slots, action_count).astype(jnp.float32), first_action
    )
    positive = allowed * (jnp.maximum(advantage, 0.0) + tremble)
    sigma = positive / jnp.sum(positive, axis=-1, keepdims=True)
    live = (jnp.arange(branch_slots)[None, :] < branch_counts[:, None]).astype(jnp.float32)
    strategy = (sigma * live[:, :, None]).reshape(par_count, branch_slots * action_count)
    branch_value = jnp.sum(sigma * advantage, axis=-1)
    history_value = jnp.sum(branch_value * live, axis=1) / branch_counts.astype(jnp.float32)
    node_count = par_count // 4
    node_onehot = (ancestor[:, None] == jnp.arange(node_count)[None, :]).astype(jnp.float32)
    ancestor_value = jnp.sum(node_onehot * history_value[:, None], axis=0)
    return (strategy, ancestor_value)


def solution(mesh):
    return jax.shard_map(
        body,
        mesh=mesh,
        in_specs=(
            P(("trav", "bulk"), None),
            P(),
            P("bulk", None),
            P(("trav", "bulk"), None),
            P(),
            P(("trav", "bulk"), None),
            P(),
            P(),
            P(),
            P(("trav", "bulk")),
            P(("trav", "bulk"), None),
            P(("trav", "bulk"), None),
            P(("trav", "bulk")),
            P(("trav", "bulk"), None),
            P(("trav", "bulk")),
        ),
        out_specs=(P(("trav", "bulk"), None), P(("trav", "bulk"))),
        check_vma=False,
    )
```

profile of v0, /device:TPU:1, one launch (start us, length us, event | category | flops | bytes accessed | tf_op | source)
XLA Modules:
  0.0 301.7 jit_solution(12102274634874806539)
XLA Ops:
  7.2 0.0 copy-start
  7.2 0.0 all-gather.6.cloned.1.call-start
  7.2 0.7 all-gather.6.cloned.1.call-update
  7.9 0.0 all-gather.4.cloned.1.call-start
  8.0 0.7 all-gather.4.cloned.1.call-update
  8.7 0.7 iota_compare_fusion.4
  9.4 0.6 reduce-window.6
  10.0 0.2 slice_reduce_fusion
  10.2 0.1 bitcast_bitcast_fusion
  10.3 0.7 fusion.12
  11.0 0.7 multiply_add_fusion
  11.7 0.8 select_reduce_fusion
  12.5 0.7 all_to_all.14
  13.2 8.6 %all-to-all-start.1 = ((s32[32,1,8]{2,1,0:T(1,128)}), s32[32,1,8]{2,1,0:T(1,128)S(1)}, u32[]{:S(2)}, u32[]{:S(2)}) async-start(s32[32,1,8]{2,1,0:T(1,128)} %bitcast.4), calls=%async_computation.1 | async-start | bytes 32768 | tf_op jit(solution)/shard_map/all_to_all | solution.py:76
  21.8 0.0 copy-start.6
  21.8 0.0 copy-start.2
  21.8 3.5 %broadcast_in_dim.48 = f32[192,4,1024]{2,1,0:T(4,128)} broadcast(bf16[192,1024]{1,0:T(8,128)(2,1)} %param.15), dimensions={0,2} | broadcast | bytes 3538944 | tf_op jit(solution)/shard_map/broadcast_in_dim | solution.py:56
  25.3 5.0 %reshape.171 = f32[768,1024]{1,0:T(8,128)} reshape(f32[192,4,1024]{2,1,0:T(4,128)} %broadcast_in_dim.48) | data formatting | bytes 6291456 | tf_op jit(solution)/shard_map/reshape | solution.py:56
  30.3 0.0 copy-done.6
  30.3 0.1 copy.55
  30.4 0.1 eq.83
  30.5 0.0 copy-done.2
  30.6 2.5 add_convert_fusion
  33.1 2.3 reshape.172
  35.3 2.2 convolution_convert_fusion
  37.5 0.0 copy-start.4
  37.6 0.0 copy-start.5
  37.6 2.6 reshape.173
  40.2 0.0 all-to-all-done.1
  40.2 7.4 %all-to-all-start = ((bf16[32,32,1024]{2,1,0:T(8,128)(2,1)}), bf16[32,32,1024]{2,1,0:T(8,128)(2,1)S(1)}, u32[]{:S(2)}, u32[]{:S(2)}) async-start(bf16[32,32,1024]{2,1,0:T(8,128)(2,1)} %reshape.173), calls=%async_computation | async-start | bytes 4194304 | tf_op jit(solution)/shard_map/all_to_all | solution.py:75
  47.6 0.0 copy-done.4
  47.6 0.1 reshape.175
  47.7 0.5 broadcast.149
  48.2 0.7 reduce.11
  48.9 0.1 reshape.174
  49.1 1.2 gather_fusion
  50.3 0.1 select_convert_fusion
  50.4 3.1 %add.100 = f32[256,4,1024]{2,1,0:T(4,128)} broadcast(f32[256,1024]{1,0:T(8,128)S(1)} %select_convert_fusion), dimensions={0,2} | broadcast | bytes 5242880 | tf_op jit(solution)/shard_map/add | solution.py:79
  53.5 5.3 %add.101 = f32[1024,1024]{1,0:T(8,128)} reshape(f32[256,4,1024]{2,1,0:T(4,128)} %add.100) | data formatting | bytes 8388608 | tf_op jit(solution)/shard_map/add | solution.py:79
  58.8 76.4 %all-gather.6.cloned.1.call-done = bf16[256,4,2048]{2,1,0:T(4,128)(2,1)} async-done(((bf16[1,4,2048]{2,1,0:T(4,128)(2,1)}), bf16[256,4,2048]{2,1,0:T(4,128)(2,1)}) %all-gather.6.cloned.1.call-update) | async-done | bytes 4194320 | tf_op jit(solution)/shard_map/all_gather | solution.py:13
  135.3 6.9 %reshape.196 = bf16[1024,2048]{1,0:T(8,128)(2,1)} reshape(bf16[256,4,2048]{2,1,0:T(4,128)(2,1)} %all-gather.6.cloned.1.call-done) | data formatting | bytes 8388608
  142.2 0.0 all-to-all-done
  142.2 111.8 %all-gather.4.cloned.1.call-done = bf16[2048,2048]{1,0:T(8,128)(2,1)} async-done(((bf16[8,2048]{1,0:T(8,128)(2,1)}), bf16[2048,2048]{1,0:T(8,128)(2,1)}) %all-gather.4.cloned.1.call-update) | async-done | bytes 8388624 | tf_op jit(solution)/shard_map/all_gather | solution.py:20
  254.0 0.0 copy-done.9
  254.1 19.9 %maximum_convert_fusion = bf16[1024,2048]{1,0:T(8,128)(2,1)} fusion(bf16[2048,2048]{1,0:T(8,128)(2,1)} %all-gather.4.cloned.1.call-done, bf16[1024,2048]{1,0:T(8,128)(2,1)} %reshape.196, f32[2048]{0:T(1024)S(1)} %copy-done.9, f32[2048]{0:T(1024)S(1)} %copy-done.10, f32[1024,1024]{1,0:T(8,128)} %add.101, bf16[1024,1024]{1,0:T(8,128)(2,1)S(1)} %bitcast.51), kind=kOutput, calls=%fused_computation.2 | convolution fusion | flops 12900630528 | bytes 23085056 | tf_op jit(solution)/shard_map/dot_general | solution.py:18
  274.0 0.0 copy-done.3
  274.0 0.0 copy-start.8
  274.0 3.4 %fusion.8 = bf16[1024,8]{0,1:T(8,128)(2,1)S(1)} fusion(bf16[1024,2048]{1,0:T(8,128)(2,1)} %maximum_convert_fusion, bf16[2048,8]{0,1:T(8,128)(2,1)S(1)} %copy-done.3, f32[8]{0:T(128)S(1)} %copy-done.7), kind=kOutput, calls=%fused_computation.13 | convolution fusion | flops 33570816 | bytes 4243488 | tf_op jit(solution)/shard_map/dot_general | solution.py:24
  277.4 0.2 copy.57
  277.6 0.3 convert_element_type.114
  277.8 0.5 broadcast.151
  278.3 0.7 reduce.12
  279.1 0.6 reshape.212
  279.7 5.8 %all-to-all-start.2 = ((bf16[32,2,128]{2,1,0:T(2,128)(2,1)}), bf16[32,2,128]{2,1,0:T(2,128)(2,1)S(1)}, u32[]{:S(2)}, u32[]{:S(2)}) async-start(bf16[32,2,128]{2,1,0:T(2,128)(2,1)} %reshape.212), calls=%async_computation.2 | async-start | bytes 32768 | tf_op jit(solution)/shard_map/all_to_all | solution.py:84
  285.5 0.1 max.35
  285.6 6.8 %all-to-all-done.2 = bf16[32,2,128]{2,1,0:T(2,128)(2,1)S(1)} async-done(((bf16[32,2,128]{2,1,0:T(2,128)(2,1)}), bf16[32,2,128]{2,1,0:T(2,128)(2,1)S(1)}, u32[]{:S(2)}, u32[]{:S(2)}) %all-to-all-start.2) | async-done | bytes 16416 | tf_op jit(solution)/shard_map/all_to_all | solution.py:84
  292.4 0.1 convert_reduce_fusion
  292.5 0.1 reshape.178
  292.6 0.7 gather_fusion.1
  293.3 0.1 copy.59
  293.3 0.1 fusion.14
  293.4 0.1 multiply_reduce_fusion
  293.6 0.6 select_reduce_fusion.1
  294.2 0.7 bitcast_multiply_fusion
  (25 shorter events, 0.2 us)
Async XLA Ops:
  7.2 41.9 %copy-start = (bf16[256,1024]{1,0:T(8,128)(2,1)S(1)}, bf16[256,1024]{1,0:T(8,128)(2,1)}, u32[]{:S(2)}) copy-start(bf16[256,1024]{1,0:T(8,128)(2,1)} %param.17) | copy-start | bytes 1572868
  7.2 128.1 %all-gather.6.cloned.1.call-start = ((), (), s32[]{:S(2)}) async-start(), calls=%async_computation.4 | async-start | bytes 4210688 | tf_op jit(solution)/shard_map/all_gather | solution.py:13
  7.9 246.1 %all-gather.4.cloned.1.call-start = ((), (), s32[]{:S(2)}) async-start(), calls=%async_computation.3 | async-start | bytes 8421376 | tf_op jit(solution)/shard_map/all_gather | solution.py:20
  13.2 27.0 %all-to-all-start.1 = ((s32[32,1,8]{2,1,0:T(1,128)}), s32[32,1,8]{2,1,0:T(1,128)S(1)}, u32[]{:S(2)}, u32[]{:S(2)}) async-start(s32[32,1,8]{2,1,0:T(1,128)} %bitcast.4), calls=%async_computation.1 | async-start | bytes 32768 | tf_op jit(solution)/shard_map/all_to_all | solution.py:76
  21.8 8.5 %copy-start.6 = (s32[192,4]{0,1:T(4,128)S(1)}, s32[192,4]{0,1:T(4,128)}, u32[]{:S(2)}) copy-start(s32[192,4]{0,1:T(4,128)} %param.25) | copy-start | bytes 9220
  21.8 8.8 %copy-start.2 = (bf16[128,1024]{1,0:T(8,128)(2,1)S(1)}, bf16[128,1024]{1,0:T(8,128)(2,1)}, u32[]{:S(2)}) copy-start(bf16[128,1024]{1,0:T(8,128)(2,1)} %param.16) | copy-start | bytes 786436
  37.5 10.0 %copy-start.4 = (s32[192,1]{0,1:T(1,128)S(1)}, s32[192,1]{0,1:T(1,128)}, u32[]{:S(2)}) copy-start(s32[192,1]{0,1:T(1,128)} %param.26) | copy-start | bytes 2308
  37.6 10.1 %copy-start.5 = (s32[192]{0:T(256)S(1)}, s32[192]{0:T(256)}, u32[]{:S(2)}) copy-start(s32[192]{0:T(256)} %param.24) | copy-start | bytes 2308
  40.2 102.0 %all-to-all-start = ((bf16[32,32,1024]{2,1,0:T(8,128)(2,1)}), bf16[32,32,1024]{2,1,0:T(8,128)(2,1)S(1)}, u32[]{:S(2)}, u32[]{:S(2)}) async-start(bf16[32,32,1024]{2,1,0:T(8,128)(2,1)} %reshape.173), calls=%async_computation | async-start | bytes 4194304 | tf_op jit(solution)/shard_map/all_to_all | solution.py:75
  58.8 195.2 %copy-start.9 = (f32[2048]{0:T(1024)S(1)}, f32[2048]{0:T(1024)}, u32[]{:S(2)}) copy-start(f32[2048]{0:T(1024)} %param.21) | copy-start | bytes 24580
  58.8 195.2 %copy-start.10 = (f32[2048]{0:T(1024)S(1)}, f32[2048]{0:T(1024)}, u32[]{:S(2)}) copy-start(f32[2048]{0:T(1024)} %param.19) | copy-start | bytes 24580
  254.1 19.9 %copy-start.3 = (bf16[2048,8]{0,1:T(8,128)(2,1)S(1)}, bf16[2048,8]{0,1:T(8,128)(2,1)}, u32[]{:S(2)}) copy-start(bf16[2048,8]{0,1:T(8,128)(2,1)} %param.22) | copy-start | bytes 98308
  254.1 19.9 %copy-start.7 = (f32[8]{0:T(128)S(1)}, f32[8]{0:T(128)}, u32[]{:S(2)}) copy-start(f32[8]{0:T(128)} %param.23) | copy-start | bytes 100
  274.0 19.3 %copy-start.1 = (s32[192,32]{0,1:T(8,128)S(1)}, s32[192,32]{0,1:T(8,128)}, u32[]{:S(2)}) copy-start(s32[192,32]{0,1:T(8,128)} %param.28) | copy-start | bytes 73732
  274.0 19.6 %copy-start.8 = (s32[192]{0:T(256)S(1)}, s32[192]{0:T(256)}, u32[]{:S(2)}) copy-start(s32[192]{0:T(256)} %param.29) | copy-start | bytes 2308
  279.7 12.7 %all-to-all-start.2 = ((bf16[32,2,128]{2,1,0:T(2,128)(2,1)}), bf16[32,2,128]{2,1,0:T(2,128)(2,1)S(1)}, u32[]{:S(2)}, u32[]{:S(2)}) async-start(bf16[32,2,128]{2,1,0:T(2,128)(2,1)} %reshape.212), calls=%async_computation.2 | async-start | bytes 32768 | tf_op jit(solution)/shard_map/all_to_all | solution.py:84
Sparse Core Ops, SparseCore 0:
  11.6 123.6 all-gather.5
  138.9 115.1 all-gather.3
where the time goes:
time: 302 us
  waiting for transfers between devices  196 us (65%)
  local copies, waits for them, and re-layouts  34.3 us (11%)
  matrix products  28 us (9%)
  starting transfers between devices  21.8 us (7%)
  between operations  14.3 us (5%)
  other arithmetic  6.85 us (2%)
    all_gather x1, waiting for transfers between devices, network(): lax.all_gather(w_second, ('trav', 'bulk'), axis=0, tiled=True)  112 us
    all_gather x1, waiting for transfers between devices, network(): lax.all_gather(w_first, ('trav', 'bulk'), axis=0, tiled=True)  76.4 us
    dot_general x1, matrix products, network(): jnp.dot(columns, lax.all_gather(w_second, ('trav', 'bulk'), axis=0, tiled...  19.9 us
    all_to_all x1, starting transfers between devices, body(): lax.all_to_all(slot_bucket, 'bulk', split_axis=0, concat_axis=0, tiled=True)  8.58 us
    add x2, local copies, waits for them, and re-layouts, body(): arrived_rows.reshape(slot_total, branch_slots, feature_count)  8.44 us
    unnamed x26, local copies, waits for them, and re-layouts  7.71 us
    all_to_all x1, starting transfers between devices, body(): lax.all_to_all(outgoing, 'bulk', split_axis=0, concat_axis=0, tiled=True)  7.38 us
    all_to_all x1, waiting for transfers between devices, body(): lax.all_to_all(evaluated.reshape(bulk_count, capacity * branch_slots * ac...  6.79 us
  transfers between devices with their start and end apart: 5, of which 3 were waited for; matrix products, arithmetic and copies ran while one was open for 13% of the time, Pallas kernels for 0%

commit v1 on v0

--- a/solution.py
+++ b/solution.py
@@ -6,12 +6,15 @@
 tremble = 0.05
 
 
+def all_by_exchange(x, axis, dim):
+    stack = jnp.stack([x] * lax.axis_size(axis))
+    return jnp.concatenate(lax.all_to_all(stack, axis, 0, 0), axis=dim)
+
+
 def network(inputs, w_first, b_first, w_second, b_second, w_head, b_head):
     columns = inputs
     first = jnp.dot(
-        columns,
-        lax.all_gather(w_first, ("trav", "bulk"), axis=0, tiled=True),
-        preferred_element_type=jnp.float32,
+        columns, all_by_exchange(w_first, ("trav", "bulk"), 0), preferred_element_type=jnp.float32
     )
     hidden_one = jnp.maximum(first + b_first, 0.0).astype(jnp.bfloat16)
     columns = hidden_one

time: 302 us -> 258 us (0.85)
  waiting for transfers between devices: 196 us -> 105 us
  blocking collectives: 0 us -> 36.7 us
  starting transfers between devices: 21.8 us -> 27.4 us
  other arithmetic: 6.85 us -> 11.5 us
    all_gather x1, waiting for transfers between devices: 112 us -> 0.01 us  [network(): lax.all_gather(w_second, ('trav', 'bulk'), axis=0, tiled=True)]
    all_to_all x1, waiting for transfers between devices: 0.01 us -> 97.1 us  [all_by_exchange(): return jnp.concatenate(lax.all_to_all(stack, axis, 0, 0), axis=dim)]
    all_gather x1 -> x0, waiting for transfers between devices: 76.4 us -> none  [network(): lax.all_gather(w_first, ('trav', 'bulk'), axis=0, tiled=True)]
    all_to_all x0 -> x1, blocking collectives: none -> 36.7 us  [body(): lax.all_to_all(outgoing, 'bulk', split_axis=0, concat_axis=0, tiled=True)]
    add x2 -> x0, local copies, waits for them, and re-layouts: 8.44 us -> none  [body(): arrived_rows.reshape(slot_total, branch_slots, feature_count)]
    unnamed x26 -> x29, local copies, waits for them, and re-layouts: 7.71 us -> 0.81 us
    reshape x0 -> x1, local copies, waits for them, and re-layouts: none -> 6.89 us  [all_by_exchange(): return jnp.concatenate(lax.all_to_all(stack, axis, 0, 0), axis=dim)]
    all_to_all x1, starting transfers between devices: 7.38 us -> 12.7 us  [all_by_exchange(): return jnp.concatenate(lax.all_to_all(stack, axis, 0, 0), axis=dim)]
  transfers between devices with their start and end apart: 5 -> 4, of which waited for: 3 -> 2; matrix products, arithmetic and copies ran while one was open for 13% -> 18% of each run, Pallas kernels for 0% -> 0%
where the time goes in v1:
time: 258 us; the launch traced here: 257 us
  waiting for transfers between devices  105 us (41%)
  blocking collectives  36.7 us (14%)
  local copies, waits for them, and re-layouts  35.1 us (14%)
  matrix products  27.9 us (11%)
  starting transfers between devices  27.4 us (11%)
  between operations  14.3 us (6%)
  other arithmetic  11.5 us (4%)
    all_to_all x1, waiting for transfers between devices, all_by_exchange(): return jnp.concatenate(lax.all_to_all(stack, axis, 0, 0), axis=dim)  97.1 us
    all_to_all x1, blocking collectives, body(): lax.all_to_all(outgoing, 'bulk', split_axis=0, concat_axis=0, tiled=True)  36.7 us
    dot_general x1, matrix products, network(): jnp.dot(columns, lax.all_gather(w_second, ('trav', 'bulk'), axis=0, tiled...  19.8 us
    all_to_all x1, starting transfers between devices, all_by_exchange(): return jnp.concatenate(lax.all_to_all(stack, axis, 0, 0), axis=dim)  12.7 us
    all_to_all x1, starting transfers between devices, body(): lax.all_to_all(slot_bucket, 'bulk', split_axis=0, concat_axis=0, tiled=True)  8.58 us
    reshape x1, local copies, waits for them, and re-layouts, all_by_exchange(): return jnp.concatenate(lax.all_to_all(stack, axis, 0, 0), axis=dim)  6.89 us
    all_to_all x1, waiting for transfers between devices, body(): lax.all_to_all(evaluated.reshape(bulk_count, capacity * branch_slots * ac...  6.79 us
    all_to_all x1, starting transfers between devices, body(): lax.all_to_all(evaluated.reshape(bulk_count, capacity * branch_slots * ac...  6.03 us
  transfers between devices with their start and end apart: 4, of which 2 were waited for; matrix products, arithmetic and copies ran while one was open for 18% of the time, Pallas kernels for 0%

profile of v1, /device:TPU:1, one launch (start us, length us, event | category | flops | bytes accessed | tf_op | source)
XLA Modules:
  0.0 257.4 jit_solution(684643269900110543)
XLA Ops:
  7.2 0.0 copy-start
  7.2 0.0 all-gather.2.cloned.1.call-start
  7.2 0.7 all-gather.2.cloned.1.call-update
  7.9 0.7 iota_compare_fusion.4
  8.6 0.6 reduce-window.6
  9.2 0.2 slice_reduce_fusion
  9.4 0.1 bitcast_bitcast_fusion
  9.5 0.7 fusion.9
  10.2 0.7 multiply_add_fusion
  10.9 0.8 select_reduce_fusion
  11.7 0.7 all_to_all.17
  12.4 8.6 %all-to-all-start.1 = ((s32[32,1,8]{2,1,0:T(1,128)}), s32[32,1,8]{2,1,0:T(1,128)S(1)}, u32[]{:S(2)}, u32[]{:S(2)}) async-start(s32[32,1,8]{2,1,0:T(1,128)} %bitcast.3), calls=%async_computation.1 | async-start | bytes 32768 | tf_op jit(solution)/shard_map/all_to_all | solution.py:79
  21.0 0.0 copy-start.8
  21.0 0.0 copy-start.3
  21.0 3.6 %broadcast_in_dim.48 = f32[192,4,1024]{2,1,0:T(4,128)} broadcast(bf16[192,1024]{1,0:T(8,128)(2,1)} %param.15), dimensions={0,2} | broadcast | bytes 3538944 | tf_op jit(solution)/shard_map/broadcast_in_dim | solution.py:59
  24.7 4.9 %reshape.190 = f32[768,1024]{1,0:T(8,128)} reshape(f32[192,4,1024]{2,1,0:T(4,128)} %broadcast_in_dim.48) | data formatting | bytes 6291456 | tf_op jit(solution)/shard_map/reshape | solution.py:59
  29.6 0.0 copy-done.8
  29.6 0.1 copy.55
  29.7 0.1 eq.83
  29.8 0.0 copy-done.3
  29.8 2.5 add_convert_fusion.1
  32.3 2.3 reshape.191
  34.6 2.2 convolution_convert_fusion
  36.8 0.0 copy-start.5
  36.9 2.6 %reshape.192 = bf16[32,32,1024]{2,1,0:T(8,128)(2,1)} reshape(bf16[256,4096]{1,0:T(8,128)(2,1)S(1)} %convolution_convert_fusion) | data formatting | bytes 4194304 | tf_op jit(solution)/shard_map/reshape | solution.py:75
  39.5 0.0 all-to-all-done.1
  39.5 36.7 %all_to_all.25 = bf16[32,32,1024]{2,1,0:T(8,128)(2,1)S(1)} all-to-all(bf16[32,32,1024]{2,1,0:T(8,128)(2,1)} %reshape.192), channel_id=1, replica_groups=mesh['trav'=8,'bulk'=32] {'bulk'}, dimensions={0} | all-to-all | bytes 4194304 | tf_op jit(solution)/shard_map/all_to_all | solution.py:78
  76.2 0.0 copy-done.5
  76.2 4.1 %stack.2 = bf16[256,4,2048]{2,1,0:T(4,128)(2,1)} broadcast(bf16[4,2048]{1,0:T(4,128)(2,1)S(1)} %copy-done.5), dimensions={1,2} | broadcast | bytes 4210688 | tf_op jit(solution)/shard_map/stack | solution.py:10
  80.3 12.7 %all-to-all-start.2 = ((bf16[256,4,2048]{2,1,0:T(4,128)(2,1)}), bf16[256,4,2048]{2,1,0:T(4,128)(2,1)}, u32[]{:S(2)}, u32[]{:S(2)}) async-start(bf16[256,4,2048]{2,1,0:T(4,128)(2,1)} %stack.2), calls=%async_computation.2 | async-start | bytes 8388608 | tf_op jit(solution)/shard_map/all_to_all | solution.py:11
  93.0 0.0 copy-done.6
  93.0 0.1 reshape.194
  93.1 0.5 broadcast.154
  93.6 0.7 reduce.11
  94.3 0.1 reshape.193
  94.5 1.2 gather_fusion
  95.6 1.1 select_convert_fusion
  96.8 3.0 %reshape.197 = f32[256,4,1024]{2,1,0:T(4,128)} reshape(bf16[32,32,1024]{2,1,0:T(8,128)(2,1)S(1)} %all_to_all.25) | data formatting | bytes 6291456 | tf_op jit(solution)/shard_map/convert_element_type | solution.py:82
  99.8 3.7 %add_convert_fusion = bf16[256,4,1024]{2,1,0:T(4,128)(2,1)S(1)} fusion(f32[256,4,1024]{2,1,0:T(4,128)} %reshape.197, f32[256,1024]{1,0:T(8,128)} %select_convert_fusion), kind=kLoop, calls=%fused_computation.9 | loop fusion | flops 2097152 | bytes 7340032 | tf_op jit(solution)/shard_map/convert_element_type | solution.py:85
  103.5 2.1 convert_element_type.119
  105.6 97.1 %all-to-all-done.2 = bf16[256,4,2048]{2,1,0:T(4,128)(2,1)} async-done(((bf16[256,4,2048]{2,1,0:T(4,128)(2,1)}), bf16[256,4,2048]{2,1,0:T(4,128)(2,1)}, u32[]{:S(2)}, u32[]{:S(2)}) %all-to-all-start.2) | async-done | bytes 4194336 | tf_op jit(solution)/shard_map/all_to_all | solution.py:11
  202.7 6.9 %reshape.195 = bf16[1024,2048]{1,0:T(8,128)(2,1)} reshape(bf16[256,4,2048]{2,1,0:T(4,128)(2,1)} %all-to-all-done.2) | data formatting | bytes 8388608 | tf_op jit(solution)/shard_map/reshape | solution.py:11
  209.6 0.0 copy-done.11
  209.6 0.0 copy-done.12
  209.6 19.8 %maximum_convert_fusion = bf16[1024,2048]{1,0:T(8,128)(2,1)} fusion(bf16[2048,2048]{1,0:T(8,128)(2,1)} %all-gather.2.cloned.1.call-done, bf16[1024,1024]{1,0:T(8,128)(2,1)S(1)} %copy-done.1, bf16[1024,2048]{1,0:T(8,128)(2,1)} %reshape.195, f32[2048]{0:T(1024)S(1)} %copy-done.11, f32[2048]{0:T(1024)S(1)} %copy-done.12), kind=kOutput, calls=%fused_computation.2 | convolution fusion | flops 12897484800 | bytes 18890752 | tf_op jit(solution)/shard_map/dot_general | solution.py:21
  229.4 0.0 copy-done.4
  229.4 0.0 copy-start.10
  229.4 3.4 %fusion.5 = bf16[1024,8]{0,1:T(8,128)(2,1)S(1)} fusion(bf16[1024,2048]{1,0:T(8,128)(2,1)} %maximum_convert_fusion, bf16[2048,8]{0,1:T(8,128)(2,1)S(1)} %copy-done.4, f32[8]{0:T(128)S(1)} %copy-done.9), kind=kOutput, calls=%fused_computation.12 | convolution fusion | flops 33570816 | bytes 4243488 | tf_op jit(solution)/shard_map/dot_general | solution.py:27
  232.8 0.2 copy.57
  233.0 0.3 convert_element_type.131
  233.3 0.5 broadcast.156
  233.8 0.7 reduce.12
  234.5 0.6 reshape.230
  235.1 6.0 %all-to-all-start.3 = ((bf16[32,2,128]{2,1,0:T(2,128)(2,1)}), bf16[32,2,128]{2,1,0:T(2,128)(2,1)S(1)}, u32[]{:S(2)}, u32[]{:S(2)}) async-start(bf16[32,2,128]{2,1,0:T(2,128)(2,1)} %reshape.230), calls=%async_computation.3 | async-start | bytes 32768 | tf_op jit(solution)/shard_map/all_to_all | solution.py:87
  241.2 0.1 max.35
  241.3 6.8 %all-to-all-done.3 = bf16[32,2,128]{2,1,0:T(2,128)(2,1)S(1)} async-done(((bf16[32,2,128]{2,1,0:T(2,128)(2,1)}), bf16[32,2,128]{2,1,0:T(2,128)(2,1)S(1)}, u32[]{:S(2)}, u32[]{:S(2)}) %all-to-all-start.3) | async-done | bytes 16416 | tf_op jit(solution)/shard_map/all_to_all | solution.py:87
  248.1 0.1 convert_reduce_fusion
  248.2 0.1 reshape.198
  248.3 0.7 gather_fusion.1
  249.0 0.1 copy.59
  249.0 0.1 fusion.11
  249.1 0.1 multiply_reduce_fusion
  249.3 0.6 select_reduce_fusion.1
  249.9 0.7 bitcast_multiply_fusion
  (29 shorter events, 0.2 us)
Async XLA Ops:
  7.2 87.3 %copy-start = (bf16[256,1024]{1,0:T(8,128)(2,1)S(1)}, bf16[256,1024]{1,0:T(8,128)(2,1)}, u32[]{:S(2)}) copy-start(bf16[256,1024]{1,0:T(8,128)(2,1)} %param.17) | copy-start | bytes 1572868
  7.2 202.4 %all-gather.2.cloned.1.call-start = ((), (), s32[]{:S(2)}) async-start(), calls=%async_computation.4 | async-start | bytes 8421376 | tf_op jit(solution)/shard_map/all_gather | solution.py:23
  12.4 27.1 %all-to-all-start.1 = ((s32[32,1,8]{2,1,0:T(1,128)}), s32[32,1,8]{2,1,0:T(1,128)S(1)}, u32[]{:S(2)}, u32[]{:S(2)}) async-start(s32[32,1,8]{2,1,0:T(1,128)} %bitcast.3), calls=%async_computation.1 | async-start | bytes 32768 | tf_op jit(solution)/shard_map/all_to_all | solution.py:79
  21.0 8.6 %copy-start.8 = (s32[192,4]{0,1:T(4,128)S(1)}, s32[192,4]{0,1:T(4,128)}, u32[]{:S(2)}) copy-start(s32[192,4]{0,1:T(4,128)} %param.25) | copy-start | bytes 9220
  21.0 8.8 %copy-start.3 = (bf16[128,1024]{1,0:T(8,128)(2,1)S(1)}, bf16[128,1024]{1,0:T(8,128)(2,1)}, u32[]{:S(2)}) copy-start(bf16[128,1024]{1,0:T(8,128)(2,1)} %param.16) | copy-start | bytes 786436
  36.8 39.3 %copy-start.5 = (bf16[4,2048]{1,0:T(4,128)(2,1)S(1)}, bf16[4,2048]{1,0:T(4,128)(2,1)}, u32[]{:S(2)}) copy-start(bf16[4,2048]{1,0:T(4,128)(2,1)} %param.18) | copy-start | bytes 49156
  80.2 12.7 %copy-start.6 = (s32[192,1]{0,1:T(1,128)S(1)}, s32[192,1]{0,1:T(1,128)}, u32[]{:S(2)}) copy-start(s32[192,1]{0,1:T(1,128)} %param.26) | copy-start | bytes 2308
  80.3 12.8 %copy-start.7 = (s32[192]{0:T(256)S(1)}, s32[192]{0:T(256)}, u32[]{:S(2)}) copy-start(s32[192]{0:T(256)} %param.24) | copy-start | bytes 2308
  80.3 122.4 %all-to-all-start.2 = ((bf16[256,4,2048]{2,1,0:T(4,128)(2,1)}), bf16[256,4,2048]{2,1,0:T(4,128)(2,1)}, u32[]{:S(2)}, u32[]{:S(2)}) async-start(bf16[256,4,2048]{2,1,0:T(4,128)(2,1)} %stack.2), calls=%async_computation.2 | async-start | bytes 8388608 | tf_op jit(solution)/shard_map/all_to_all | solution.py:11
  105.6 104.0 %copy-start.1 = (bf16[1024,1024]{1,0:T(8,128)(2,1)S(1)}, bf16[1024,1024]{1,0:T(8,128)(2,1)}, u32[]{:S(2)}) copy-start(bf16[1024,1024]{1,0:T(8,128)(2,1)} %convert_element_type.119) | copy-start | bytes 6291460
  105.6 104.0 %copy-start.11 = (f32[2048]{0:T(1024)S(1)}, f32[2048]{0:T(1024)}, u32[]{:S(2)}) copy-start(f32[2048]{0:T(1024)} %param.21) | copy-start | bytes 24580
  105.6 104.0 %copy-start.12 = (f32[2048]{0:T(1024)S(1)}, f32[2048]{0:T(1024)}, u32[]{:S(2)}) copy-start(f32[2048]{0:T(1024)} %param.19) | copy-start | bytes 24580
  209.6 19.8 %copy-start.4 = (bf16[2048,8]{0,1:T(8,128)(2,1)S(1)}, bf16[2048,8]{0,1:T(8,128)(2,1)}, u32[]{:S(2)}) copy-start(bf16[2048,8]{0,1:T(8,128)(2,1)} %param.22) | copy-start | bytes 98308
  209.6 19.8 %copy-start.9 = (f32[8]{0:T(128)S(1)}, f32[8]{0:T(128)}, u32[]{:S(2)}) copy-start(f32[8]{0:T(128)} %param.23) | copy-start | bytes 100
  229.4 19.6 %copy-start.2 = (s32[192,32]{0,1:T(8,128)S(1)}, s32[192,32]{0,1:T(8,128)}, u32[]{:S(2)}) copy-start(s32[192,32]{0,1:T(8,128)} %param.28) | copy-start | bytes 73732
  229.4 19.8 %copy-start.10 = (s32[192]{0:T(256)S(1)}, s32[192]{0:T(256)}, u32[]{:S(2)}) copy-start(s32[192]{0:T(256)} %param.29) | copy-start | bytes 2308
  235.1 12.9 %all-to-all-start.3 = ((bf16[32,2,128]{2,1,0:T(2,128)(2,1)}), bf16[32,2,128]{2,1,0:T(2,128)(2,1)S(1)}, u32[]{:S(2)}, u32[]{:S(2)}) async-start(bf16[32,2,128]{2,1,0:T(2,128)(2,1)} %reshape.230), calls=%async_computation.3 | async-start | bytes 32768 | tf_op jit(solution)/shard_map/all_to_all | solution.py:87
Sparse Core Ops, SparseCore 0:
  11.6 145.7 all-gather.1
